TPU v7x, 128 devices: a whole 4x4x4 slice. The times are simulated.
128 devices in a mesh: gr: 16 (over x, y), gc: 8 (over z, core).
Axes of the slice: x: 4, y: 4, z: 4, core: 2. Of those that a mesh axis runs over, the one named last changes fastest.
Arguments:
- child_rows: float32 [8192, 12288], P('gr', 'gc'), may hold values from -1.5 to 1.5
- row_map: int32 [8192], P('gr'), may hold values from 0 to 8191, as said below
- stair: int32 [64], replicated, may hold values from 0 to 896, as said below
Outputs:
- factor: float32 [1024, 12288], P('gr', 'gc')
- projected: float32 [8192, 12288], P('gr', 'gc')
Inputs may be any that keep to these rules, and one draw needn't show every extreme that they name: row_map is a permutation of 0 to 8191. Of the 512 rows of one index of gr, at most 152 go to the rows of any one index of gr (row_map // 512), and some index of gr sends exactly 152 to one index. stair is nondecreasing and a multiple of 128; the first quarter of the blocks is 0 and the last block holds 896.
All inputs are finite; a program needn't handle non-finite values.
Results may differ from a plain program's by a relative error of at most 0.0003.
Values sent between devices are 32-bit elements; how exact they have to be, the bound alone decides.
A program may use at most 128 MiB of HBM per device.

v0:
```python
import jax
import jax.numpy as jnp
from jax import lax
from jax.sharding import PartitionSpec as P

PANEL = 512
NPANEL = 2
STAIR_BLOCK = 128


def spread(value, axis, source):
    kept = jnp.where(lax.axis_index(axis) == source, value, 0).astype(value.dtype)
    return lax.psum(kept, axis)


def pack_rows(values, targets, groups):
    rows_dev = values.shape[0]
    base_rows = 3 * rows_dev // (4 * groups)
    capacity = rows_dev - base_rows * (groups - 1)
    target_dev = targets // rows_dev
    target_row = targets % rows_dev
    onehot = (target_dev[:, None] == jnp.arange(groups, dtype=jnp.int32)[None, :]).astype(jnp.int32)
    rank_within = jnp.sum((jnp.cumsum(onehot, axis=0) - onehot) * onehot, axis=1)
    buffer_index = target_dev * capacity + rank_within
    source_row = (
        jnp.full((groups * capacity,), rows_dev, jnp.int32)
        .at[buffer_index]
        .set(jnp.arange(rows_dev, dtype=jnp.int32))
    )
    sent_rows = jnp.take(values, source_row, axis=0, mode="fill", fill_value=0.0)
    sent_slots = (
        jnp.full((groups * capacity,), rows_dev, jnp.int32).at[buffer_index].set(target_row)
    )
    return (
        sent_rows.reshape(groups, capacity, values.shape[1]),
        sent_slots.reshape(groups, capacity),
    )


def place_rows(recv_rows, recv_slots, rows_dev):
    flat_rows = recv_rows.reshape(-1, recv_rows.shape[-1])
    flat_slots = recv_slots.reshape(-1)
    where_from = (
        jnp.zeros((rows_dev,), jnp.int32)
        .at[flat_slots]
        .set(jnp.arange(flat_slots.shape[0], dtype=jnp.int32), mode="drop")
    )
    return jnp.take(flat_rows, where_from, axis=0)


def matmul(left, right):
    return jnp.dot(left, right, precision=lax.Precision.HIGHEST, preferred_element_type=jnp.float32)


def shards(child_rows, row_map, stair):
    groups = lax.axis_size("gr")
    rows_dev, cols_dev = child_rows.shape
    columns = lax.axis_index("gc") * cols_dev + jnp.arange(cols_dev, dtype=jnp.int32)
    sent_rows, sent_slots = pack_rows(child_rows, row_map, groups)
    recv_rows, recv_slots = (
        lax.all_to_all(sent_rows, "gr", split_axis=0, concat_axis=0, tiled=True),
        lax.all_to_all(sent_slots, "gr", split_axis=0, concat_axis=0, tiled=True),
    )
    front_work = place_rows(recv_rows, recv_slots, rows_dev)
    own_rows = lax.axis_index("gr") * rows_dev + jnp.arange(rows_dev, dtype=jnp.int32)
    limits = jnp.take(stair, own_rows // STAIR_BLOCK)
    front_work = jnp.where(
        columns[None, :] >= limits[:, None], front_work, jnp.zeros_like(front_work)
    )
    blocks = []
    for step in range(NPANEL):
        panel_block = spread(front_work[:, step * PANEL : (step + 1) * PANEL], "gc", 0)
        gram_one = lax.psum(matmul(panel_block.T, panel_block), "gr")
        lower_one = jnp.linalg.cholesky(gram_one)
        basis_cols = jax.scipy.linalg.solve_triangular(lower_one, panel_block.T, lower=True).T
        coupling = lax.psum(matmul(basis_cols.T, front_work), "gr")
        front_work = front_work - matmul(basis_cols, coupling)
        blocks.append(coupling)
    stacked = jnp.concatenate(blocks, axis=0)
    share_rows = stacked.shape[0] // groups
    factor = lax.dynamic_slice_in_dim(stacked, lax.axis_index("gr") * share_rows, share_rows, 0)
    return (factor, front_work)


def solution(mesh):
    placed = (P("gr", "gc"), P("gr"), P())
    return jax.shard_map(
        shards,
        mesh=mesh,
        in_specs=placed,
        out_specs=(P("gr", "gc"), P("gr", "gc")),
        check_vma=False,
    )
```

profile of v0, /device:TPU:1, one launch (start us, length us, event | category | flops | bytes accessed | tf_op | source)
XLA Modules:
  0.0 1196.0 jit_solution(4208776243515195790)
XLA Ops:
  9.6 2.5 scatter_custom_fusion
  12.7 7.6 all-to-all-start
  20.3 2.5 scatter_custom_fusion.2
  23.0 10.1 gather_fusion
  33.1 11.6 broadcast_select_fusion
  44.7 6.8 all-to-all-start.1
  54.2 4.4 compare_select_fusion.3
  60.1 35.7 %select_select_fusion.3 = s32[512]{0:T(512)S(1)} fusion(pred[512]{0:T(512)(128)(4,1)S(1)} %get-tuple-element.130, pred[512]{0:T(512)(128)(4,1)S(1)} %get-tuple-element.131, pred[512]{0:T(512)(128)(4,1)S(1)} %get-tuple-element.132, pred[512]{0:T(512)(128)(4,1)S(1)} %get-tuple-element.133, pred[512]{0:T(512)(128)(4,1)S(1)} %get-tuple-element.134, ...), kind=kLoop, calls=%fused_computation.224 | loop fusion | flops 40960 | bytes 33512 | tf_op jit(solution)/shard_map/jit(_take)/select_n | solution.py:66
  96.0 12.3 %scatter_custom_fusion.1 = s32[512]{0:T(512)S(1)} fusion(s32[2432]{0:T(1024)S(1)} %fusion.63, s32[2432]{0:T(1024)S(1)} %iota.86, s32[]{:T(128)} %constant.193.clone.1), kind=kCustom, calls=%fused_computation.249 | custom fusion | bytes 2052 | tf_op jit(solution)/shard_map/scatter | solution.py:46
  108.4 204.8 %all-to-all-done.1 = f32[16,152,1536]{2,1,0:T(8,128)} async-done(((f32[16,152,1536]{2,1,0:T(8,128)}), f32[16,152,1536]{2,1,0:T(8,128)}, u32[]{:S(2)}, u32[]{:S(2)}) %all-to-all-start.1) | async-done | bytes 14942240 | tf_op jit(solution)/shard_map/all_to_all | solution.py:61
  313.2 9.8 gather_fusion.1
  323.0 2.3 select_select_fusion
  326.5 69.1 %all-reduce.8.cloned.1.call-done = f32[512,512]{1,0:T(8,128)} async-done(((f32[512,512]{1,0:T(8,128)}), f32[512,512]{1,0:T(8,128)}) %all-reduce.8.cloned.1.call-update) | async-done | bytes 1048592 | tf_op jit(solution)/shard_map/psum | solution.py:13
  395.6 4.4 fusion.88
  400.5 86.2 %all-reduce.10.cloned.1.call-done = f32[512,512]{0,1:T(8,128)} async-done(((f32[512,512]{0,1:T(8,128)}), f32[512,512]{0,1:T(8,128)}) %all-reduce.10.cloned.1.call-update) | async-done | bytes 1048592 | tf_op jit(solution)/shard_map/psum | solution.py:73
  486.7 2.5 copy.11
  492.0 11.7 cholesky.286
  504.9 9.8 custom-call.27
  517.9 11.7 cholesky.305
  530.3 10.0 custom-call.28
  542.6 11.7 cholesky.326
  554.9 9.8 custom-call.29
  567.0 11.7 cholesky.343
  584.6 2.7 select_select_fusion.2
  587.3 11.7 while.4
  599.0 39.9 %custom-call.30 = f32[4,128,128]{1,2,0:T(8,128)} custom-call(f32[4,128,128]{2,1,0:T(8,128)S(1)} %get-tuple-element.18), custom_call_target="InvertDiagBlocksLowerTriangular" | custom-call | tf_op jit(solution)/shard_map/jit(_solve_triangular)/triangular_solve | solution.py:75
  645.9 2.6 convolution_subtract_fusion.7
  649.7 6.9 fusion.13
  656.6 96.0 %all-reduce.12.cloned.1.call-done = f32[512,1536]{1,0:T(8,128)} async-done(((f32[512,1536]{1,0:T(8,128)}), f32[512,1536]{1,0:T(8,128)}) %all-reduce.12.cloned.1.call-update) | async-done | bytes 3145744 | tf_op jit(solution)/shard_map/psum | solution.py:76
  752.6 7.8 convolution_subtract_fusion.1
  761.7 60.2 %all-reduce.14.cloned.1.call-done = f32[512,512]{1,0:T(8,128)} async-done(((f32[512,512]{1,0:T(8,128)}), f32[512,512]{1,0:T(8,128)}) %all-reduce.14.cloned.1.call-update) | async-done | bytes 1048592 | tf_op jit(solution)/shard_map/psum | solution.py:13
  821.9 4.5 fusion.89
  826.7 86.5 %all-reduce.16.cloned.1.call-done = f32[512,512]{0,1:T(8,128)} async-done(((f32[512,512]{0,1:T(8,128)}), f32[512,512]{0,1:T(8,128)}) %all-reduce.16.cloned.1.call-update) | async-done | bytes 1048592 | tf_op jit(solution)/shard_map/psum | solution.py:73
  913.1 2.5 copy.13
  918.4 11.7 cholesky.358
  931.3 9.8 custom-call.31
  944.3 11.7 cholesky.377
  956.6 10.0 custom-call.32
  969.0 11.7 cholesky.398
  981.3 9.8 custom-call.33
  993.4 11.7 cholesky.415
  1011.0 2.7 select_select_fusion.1
  1013.8 11.8 while.5
  1025.5 39.9 %custom-call.34 = f32[4,128,128]{1,2,0:T(8,128)} custom-call(f32[4,128,128]{2,1,0:T(8,128)S(1)} %get-tuple-element.19), custom_call_target="InvertDiagBlocksLowerTriangular" | custom-call | tf_op jit(solution)/shard_map/jit(_solve_triangular)/triangular_solve | solution.py:75
  1072.4 2.6 convolution_subtract_fusion.6
  1076.2 6.9 fusion.12
  1083.1 95.9 %all-reduce.18.cloned.1.call-done = f32[512,1536]{1,0:T(8,128)} async-done(((f32[512,1536]{1,0:T(8,128)}), f32[512,1536]{1,0:T(8,128)}) %all-reduce.18.cloned.1.call-update) | async-done | bytes 3145744 | tf_op jit(solution)/shard_map/psum | solution.py:76
  1179.0 9.2 convolution_subtract_fusion
  (183 shorter events, 83.5 us)
Async XLA Ops:
  7.2 15.8 %copy-start = (f32[512,1536]{1,0:T(8,128)S(1)}, f32[512,1536]{1,0:T(8,128)}, u32[]{:S(2)}) copy-start(f32[512,1536]{1,0:T(8,128)} %param.6) | copy-start | bytes 9437188
  12.7 32.0 %all-to-all-start = ((s32[16,1,152]{2,1,0:T(1,128)}), s32[16,1,152]{2,1,0:T(1,128)S(1)}, u32[]{:S(2)}, u32[]{:S(2)}) async-start(s32[16,1,152]{2,1,0:T(1,128)} %all_to_all.9), calls=%async_computation | async-start | bytes 32768 | tf_op jit(solution)/shard_map/all_to_all | solution.py:62
  44.7 8.1 copy-start.14
  44.7 268.5 %all-to-all-start.1 = ((f32[16,152,1536]{2,1,0:T(8,128)}), f32[16,152,1536]{2,1,0:T(8,128)}, u32[]{:S(2)}, u32[]{:S(2)}) async-start(f32[16,152,1536]{2,1,0:T(8,128)} %broadcast_select_fusion), calls=%async_computation.1 | async-start | bytes 29884416 | tf_op jit(solution)/shard_map/all_to_all | solution.py:61
  51.5 344.0 %all-reduce.8.cloned.1.call-start = ((), (), s32[]{:S(2)}) async-start(), calls=%async_computation.2 | async-start | bytes 2097152 | tf_op jit(solution)/shard_map/psum | solution.py:13
  325.3 323.6 %copy-start.3 = (f32[512,1536]{1,0:T(8,128)}, f32[512,1536]{1,0:T(8,128)S(1)}, u32[]{:S(2)}) copy-start(f32[512,1536]{1,0:T(8,128)S(1)} %select_select_fusion) | copy-start | bytes 9437188
  326.5 160.2 %all-reduce.10.cloned.1.call-start = ((), (), s32[]{:S(2)}) async-start(), calls=%async_computation.3 | async-start | bytes 2097152 | tf_op jit(solution)/shard_map/psum | solution.py:73
  400.0 352.6 %all-reduce.12.cloned.1.call-start = ((), (), s32[]{:S(2)}) async-start(), calls=%async_computation.4 | async-start | bytes 6291456 | tf_op jit(solution)/shard_map/psum | solution.py:76
  491.0 1.0 copy-start.10
  639.0 6.4 copy-start.15
  643.3 5.6 copy-start.7
  645.9 3.1 copy-start.9
  648.9 0.7 copy-start.13
  656.6 165.3 %all-reduce.14.cloned.1.call-start = ((), (), s32[]{:S(2)}) async-start(), calls=%async_computation.5 | async-start | bytes 2097152 | tf_op jit(solution)/shard_map/psum | solution.py:13
  760.4 315.0 %copy-start.2 = (f32[512,1536]{1,0:T(8,128)}, f32[512,1536]{1,0:T(8,128)S(1)}, u32[]{:S(2)}) copy-start(f32[512,1536]{1,0:T(8,128)S(1)} %convolution_subtract_fusion.1) | copy-start | bytes 9437188
  761.6 151.5 %all-reduce.16.cloned.1.call-start = ((), (), s32[]{:S(2)}) async-start(), calls=%async_computation.6 | async-start | bytes 2097152 | tf_op jit(solution)/shard_map/psum | solution.py:73
  826.4 352.6 %all-reduce.18.cloned.1.call-start = ((), (), s32[]{:S(2)}) async-start(), calls=%async_computation.7 | async-start | bytes 6291456 | tf_op jit(solution)/shard_map/psum | solution.py:76
  917.4 1.0 copy-start.11
  1065.5 6.4 copy-start.16
  1069.8 5.6 copy-start.6
  1072.4 3.1 copy-start.8
  1075.5 0.7 copy-start.12
  1179.0 9.2 copy-start.4
  1179.0 9.2 copy-start.5
  1179.0 10.0 copy-start.1
Sparse Core Ops, SparseCore 0:
  326.6 68.9 all-reduce.7
  400.1 86.5 all-reduce.9
  656.7 95.8 all-reduce.11
  761.7 60.1 all-reduce.13
  826.6 86.5 all-reduce.15
  1083.2 95.7 all-reduce.17
where the time goes:
time: 1210 us; the launch traced here: 1200 us
  waiting for transfers between devices  699 us (58%)
  other arithmetic  312 us (26%)
  local copies, waits for them, and re-layouts  75.2 us (6%)
  matrix products  74.9 us (6%)
  between operations  20.1 us (2%)
  starting transfers between devices  15.3 us (1%)
    all_to_all x1, waiting for transfers between devices, shards(): lax.all_to_all(sent_rows, 'gr', split_axis=0, concat_axis=0, tiled=True)  205 us
    psum x2, waiting for transfers between devices, shards(): coupling = lax.psum(matmul(basis_cols.T, front_work), 'gr')  192 us
    psum x2, waiting for transfers between devices, shards(): gram_one = lax.psum(matmul(panel_block.T, panel_block), 'gr')  173 us
    another operation x30, other arithmetic, shards(): lower_one = jnp.linalg.cholesky(gram_one)  162 us
    psum x2, waiting for transfers between devices, spread(): return lax.psum(kept, axis)  129 us
    another operation x5, other arithmetic, shards(): jax.scipy.linalg.solve_triangular(lower_one, panel_block.T, lower=True)  85.3 us
    dot_general x6, matrix products, matmul(): jnp.dot(left, right, precision=lax.Precision.HIGHEST, preferred_element_t...  39.7 us
    select_n x1, other arithmetic, shards(): limits = jnp.take(stair, own_rows // STAIR_BLOCK)  35.7 us
  transfers between devices with their start and end apart: 8, of which 7 were waited for; matrix products, arithmetic and copies ran while one was open for 7% of the time, Pallas kernels for 0%

commit v1 on v0

--- a/solution.py
+++ b/solution.py
@@ -52,34 +52,69 @@
     return jnp.dot(left, right, precision=lax.Precision.HIGHEST, preferred_element_type=jnp.float32)
 
 
+def high(left, right, contract):
+    return lax.dot_general(
+        left, right, (contract, ((), ())), precision=lax.Precision.HIGH,
+        preferred_element_type=jnp.float32,
+    )
+
+
+def cholesky_inverse(gram):
+    lower = jnp.linalg.cholesky(gram)
+    eye = jnp.eye(gram.shape[0], dtype=gram.dtype)
+    return jax.scipy.linalg.solve_triangular(lower, eye, lower=True)
+
+
+def gram_inverse_factor(g00, g10, g11):
+    i00 = cholesky_inverse(g00)
+    l10 = matmul(g10, i00.T)
+    i11 = cholesky_inverse(g11 - matmul(l10, l10.T))
+    i10 = -matmul(i11, matmul(l10, i00))
+    return jnp.concatenate(
+        [jnp.concatenate([i00, jnp.zeros_like(i00)], 1), jnp.concatenate([i10, i11], 1)], 0
+    )
+
+
 def shards(child_rows, row_map, stair):
     groups = lax.axis_size("gr")
     rows_dev, cols_dev = child_rows.shape
+    wide = NPANEL * PANEL
+    half = PANEL // 2
     columns = lax.axis_index("gc") * cols_dev + jnp.arange(cols_dev, dtype=jnp.int32)
-    sent_rows, sent_slots = pack_rows(child_rows, row_map, groups)
+    limits = jnp.take(stair, row_map // STAIR_BLOCK)
+    masked = jnp.where(columns[None, :] >= limits[:, None], child_rows, jnp.zeros_like(child_rows))
+
+    own = masked[:, :wide]
+    left = matmul(own.T, own[:, :PANEL])
+    low = matmul(own[:, PANEL:].T, own[:, PANEL:])
+    low = jnp.concatenate([low[:, :half], low[:, half:]], axis=0)
+    gram = jnp.concatenate([left, low], axis=1)
+    gram = jnp.where(lax.axis_index("gc") == 0, gram, jnp.zeros_like(gram))
+    gram, masked, own = lax.optimization_barrier((gram, masked, own))
+    gram = lax.psum(gram, ("gr", "gc"))
+
+    sent_rows, sent_slots = pack_rows(masked, row_map, groups)
     recv_rows, recv_slots = (
         lax.all_to_all(sent_rows, "gr", split_axis=0, concat_axis=0, tiled=True),
         lax.all_to_all(sent_slots, "gr", split_axis=0, concat_axis=0, tiled=True),
     )
-    front_work = place_rows(recv_rows, recv_slots, rows_dev)
-    own_rows = lax.axis_index("gr") * rows_dev + jnp.arange(rows_dev, dtype=jnp.int32)
-    limits = jnp.take(stair, own_rows // STAIR_BLOCK)
-    front_work = jnp.where(
-        columns[None, :] >= limits[:, None], front_work, jnp.zeros_like(front_work)
-    )
-    blocks = []
-    for step in range(NPANEL):
-        panel_block = spread(front_work[:, step * PANEL : (step + 1) * PANEL], "gc", 0)
-        gram_one = lax.psum(matmul(panel_block.T, panel_block), "gr")
-        lower_one = jnp.linalg.cholesky(gram_one)
-        basis_cols = jax.scipy.linalg.solve_triangular(lower_one, panel_block.T, lower=True).T
-        coupling = lax.psum(matmul(basis_cols.T, front_work), "gr")
-        front_work = front_work - matmul(basis_cols, coupling)
-        blocks.append(coupling)
-    stacked = jnp.concatenate(blocks, axis=0)
-    share_rows = stacked.shape[0] // groups
+    own, gram = lax.optimization_barrier((own, gram))
+    panel = spread(own, "gc", 0)
+    local = high(panel, masked, ((0,), (0,)))
+    products = lax.psum(local, "gr")
+
+    low = jnp.concatenate([gram[:PANEL, PANEL:], gram[PANEL:, PANEL:]], axis=1)
+    inverse = gram_inverse_factor(gram[:PANEL, :PANEL], gram[PANEL:, :PANEL], low)
+
+    front = place_rows(recv_rows, recv_slots, rows_dev)
+    front_own, _ = lax.optimization_barrier((front[:, :wide], local))
+    front_panel = spread(front_own, "gc", 0)
+    basis = high(front_panel, inverse, ((1,), (1,)))
+    stacked = high(inverse, products, ((1,), (0,)))
+    projected = front - high(basis, stacked, ((1,), (0,)))
+    share_rows = wide // groups
     factor = lax.dynamic_slice_in_dim(stacked, lax.axis_index("gr") * share_rows, share_rows, 0)
-    return (factor, front_work)
+    return (factor, projected)
 
 
 def solution(mesh):

time: 1210 us -> 972 us (0.80)
  waiting for transfers between devices: 699 us -> 430 us
  matrix products: 74.9 us -> 89.4 us
    all_to_all x1, waiting for transfers between devices: 205 us -> 0.01 us  [shards(): lax.all_to_all(sent_rows, 'gr', split_axis=0, concat_axis=0, tiled=True)]
    psum x2, waiting for transfers between devices: 129 us -> 45.4 us  [spread(): return lax.psum(kept, axis)]
    dot_general x0 -> x4, matrix products: none -> 39.7 us  [high(): lax.dot_general(left, right, (contract, ((), ())), precision=lax.Precisio...]
    dot_general x6, matrix products: 39.7 us -> 18.9 us  [matmul(): jnp.dot(left, right, precision=lax.Precision.HIGHEST, preferred_element_t...]
    psum x4 -> x2, waiting for transfers between devices: 365 us -> 384 us  [the longest x1 374 us: shards(): gram = lax.psum(gram, ('gr', 'gc'))]
    select_n x2 -> x3, other arithmetic: 38 us -> 44.6 us  [the longest x1 40.5 us: shards(): limits = jnp.take(stair, row_map // STAIR_BLOCK)]
  transfers between devices with their start and end apart: 8 -> 6, of which waited for: 7 -> 3; matrix products, arithmetic and copies ran while one was open for 7% -> 47% of each run, Pallas kernels for 0% -> 0%
where the time goes in v1:
time: 972 us; the launch traced here: 960 us
  waiting for transfers between devices  430 us (44%)
  other arithmetic  320 us (33%)
  matrix products  89.4 us (9%)
  local copies, waits for them, and re-layouts  85.2 us (9%)
  between operations  20 us (2%)
  starting transfers between devices  14.6 us (2%)
    psum x1, waiting for transfers between devices, shards(): gram = lax.psum(gram, ('gr', 'gc'))  374 us
    another operation x29, other arithmetic, cholesky_inverse(): lower = jnp.linalg.cholesky(gram)  166 us
    another operation x6, other arithmetic, cholesky_inverse(): return jax.scipy.linalg.solve_triangular(lower, eye, lower=True)  87.6 us
    psum x2, waiting for transfers between devices, spread(): return lax.psum(kept, axis)  45.4 us
    select_n x1, other arithmetic, shards(): limits = jnp.take(stair, row_map // STAIR_BLOCK)  40.5 us
    dot_general x4, matrix products, high(): lax.dot_general(left, right, (contract, ((), ())), precision=lax.Precisio...  39.7 us
    another operation x27, local copies, waits for them, and re-layouts, cholesky_inverse(): return jax.scipy.linalg.solve_triangular(lower, eye, lower=True)  26 us
  transfers between devices with their start and end apart: 6, of which 3 were waited for; matrix products, arithmetic and copies ran while one was open for 47% of the time, Pallas kernels for 0%

profile of v1, /device:TPU:1, one launch (start us, length us, event | category | flops | bytes accessed | tf_op | source)
XLA Modules:
  0.0 959.6 jit_solution(5072844450119974676)
XLA Ops:
  9.4 2.5 scatter_custom_fusion
  12.6 7.6 all-to-all-start
  28.0 40.5 %select_select_fusion.2 = s32[512]{0:T(512)S(1)} fusion(s32[512]{0:T(512)} %param.7, s32[]{:T(128)} %bitcast, s32[]{:T(128)} %bitcast.1, s32[]{:T(128)} %bitcast.2, s32[]{:T(128)} %bitcast.3, s32[]{:T(128)} %bitcast.4, s32[]{:T(128)} %bitcast.5, s32[]{:T(128)} %bitcast.6, s32[]{:T(128)} %bitcast.7, s32[]{:T(128)} %bitcast.8, s32[]{:T(128)} %bitcast.9, ...), kind=kLoop, calls=%fused_computation.171 | loop fusion | flops 75776 | bytes 4352 | tf_op jit(solution)/shard_map/jit(_take)/select_n | solution.py:84
  70.7 2.9 fusion.2
  73.6 4.9 fusion.4
  78.5 2.5 scatter_custom_fusion.2
  84.9 10.1 %gather_fusion = f32[2432,1536]{1,0:T(8,128)} fusion(f32[512,1536]{1,0:T(8,128)S(1)} %compare_select_fusion, s32[3072]{0:T(1024)S(1)} %pad_clamp_fusion), kind=kCustom, calls=%fused_computation | custom fusion | bytes 29894144 | tf_op jit(solution)/shard_map/jit(_take)/gather | solution.py:30
  95.0 11.6 %broadcast_select_fusion = f32[16,152,1536]{2,1,0:T(8,128)} fusion(f32[16,152,1536]{2,1,0:T(8,128)} %bitcast.192, pred[16,152]{1,0:T(8,128)(4,1)S(1)} %broadcast_in_dim.63), kind=kLoop, calls=%fused_computation.9 | loop fusion | flops 3735552 | bytes 29886848 | tf_op jit(solution)/shard_map/jit(_take)/select_n | solution.py:30
  106.6 6.7 all-to-all-start.1
  114.4 12.8 %scatter_custom_fusion.1 = s32[512]{0:T(512)S(1)} fusion(s32[2432]{0:T(1024)S(1)} %fusion.76, s32[2432]{0:T(1024)S(1)} %iota.96, s32[]{:T(128)} %copy.55), kind=kCustom, calls=%fused_computation.190 | custom fusion | bytes 2052 | tf_op jit(solution)/shard_map/scatter | solution.py:46
  127.3 373.6 %all-reduce.7.cloned.1.call-done = f32[1024,768]{0,1:T(8,128)} async-done(((f32[1024,768]{0,1:T(8,128)}), f32[1024,768]{0,1:T(8,128)}) %all-reduce.7.cloned.1.call-update) | async-done | bytes 3145744 | tf_op jit(solution)/shard_map/psum | solution.py:94
  503.9 11.7 %cholesky.286 = f32[128,128]{1,0:T(8,128)S(1)} custom-call(f32[128,128]{1,0:T(8,128)S(1)} %cholesky.426), custom_call_target="Cholesky" | custom-call | tf_op jit(solution)/shard_map/jit(cholesky)/cholesky | solution.py:63
  516.8 9.8 %custom-call.27 = f32[1,128,128]{1,2,0:T(8,128)S(1)} custom-call(f32[1,128,128]{2,1,0:T(8,128)S(1)} %get-tuple-element.75), custom_call_target="InvertDiagBlocksLowerTriangular" | custom-call | tf_op jit(solution)/shard_map/jit(cholesky)/cholesky | solution.py:63
  529.0 11.7 %cholesky.305 = f32[128,128]{1,0:T(8,128)S(1)} custom-call(f32[128,128]{1,0:T(8,128)S(1)} %cholesky.430), custom_call_target="Cholesky" | custom-call | tf_op jit(solution)/shard_map/jit(cholesky)/cholesky | solution.py:63
  541.4 10.0 %custom-call.28 = f32[1,128,128]{1,2,0:T(8,128)S(1)} custom-call(f32[1,128,128]{2,1,0:T(8,128)S(1)} %get-tuple-element.72), custom_call_target="InvertDiagBlocksLowerTriangular" | custom-call | tf_op jit(solution)/shard_map/jit(cholesky)/cholesky | solution.py:63
  553.7 11.7 %cholesky.326 = f32[128,128]{1,0:T(8,128)S(1)} custom-call(f32[128,128]{1,0:T(8,128)S(1)} %cholesky.435), custom_call_target="Cholesky" | custom-call | tf_op jit(solution)/shard_map/jit(cholesky)/cholesky | solution.py:63
  566.1 9.8 %custom-call.29 = f32[1,128,128]{1,2,0:T(8,128)S(1)} custom-call(f32[1,128,128]{2,1,0:T(8,128)S(1)} %get-tuple-element.69), custom_call_target="InvertDiagBlocksLowerTriangular" | custom-call | tf_op jit(solution)/shard_map/jit(cholesky)/cholesky | solution.py:63
  578.2 11.7 %cholesky.343 = f32[128,128]{1,0:T(8,128)S(1)} custom-call(f32[128,128]{1,0:T(8,128)S(1)} %convolution_subtract_fusion.13), custom_call_target="Cholesky" | custom-call | tf_op jit(solution)/shard_map/jit(cholesky)/cholesky | solution.py:63
  595.3 2.3 select_select_fusion.1
  597.7 11.8 %while.4 = (s32[]{:T(128)}, f32[512,512]{1,0:T(8,128)}, s32[4,2]{0,1:T(2,128)S(1)}, f32[4,128,128]{2,1,0:T(8,128)S(1)}, s32[]{:T(128)}) while((s32[]{:T(128)}, f32[512,512]{1,0:T(8,128)}, s32[4,2]{0,1:T(2,128)S(1)}, f32[4,128,128]{2,1,0:T(8,128)S(1)}, s32[]{:T(128)}) %tuple.124), condition=%wide.while_cond, body=%wide.while_body.sunk | while | flops 2 | bytes 131181 | solution.py:65
  601.3 2.3 bitcast_dynamic-update-slice_fusion.4
  604.3 2.3 bitcast_dynamic-update-slice_fusion.4
  609.5 39.9 %custom-call.30 = f32[4,128,128]{1,2,0:T(8,128)} custom-call(f32[4,128,128]{2,1,0:T(8,128)S(1)} %get-tuple-element.30), custom_call_target="InvertDiagBlocksLowerTriangular" | custom-call | tf_op jit(solution)/shard_map/jit(_solve_triangular)/triangular_solve | solution.py:65
  658.1 3.6 fusion.15
  662.7 2.9 convolution_subtract_fusion.1
  665.5 2.6 copy.15
  668.2 45.4 %all-reduce.9.cloned.1.call-done = f32[512,1024]{1,0:T(8,128)} async-done(((f32[512,1024]{1,0:T(8,128)}), f32[512,1024]{1,0:T(8,128)}) %all-reduce.9.cloned.1.call-update) | async-done | bytes 2097168 | tf_op jit(solution)/shard_map/psum | solution.py:13
  713.5 9.2 fusion.105
  722.7 9.8 %gather_fusion.1 = f32[512,1536]{1,0:T(8,128)} fusion(f32[2432,1536]{1,0:T(8,128)} %bitcast.89, s32[1024]{0:T(1024)S(1)} %pad_clamp_fusion.1), kind=kCustom, calls=%fused_computation.1 | custom fusion | bytes 6293504 | tf_op jit(solution)/shard_map/jit(_take)/gather | solution.py:48
  739.4 11.7 %cholesky.358 = f32[128,128]{1,0:T(8,128)S(1)} custom-call(f32[128,128]{1,0:T(8,128)S(1)} %cholesky.439), custom_call_target="Cholesky" | custom-call | tf_op jit(solution)/shard_map/jit(cholesky)/cholesky | solution.py:63
  752.3 9.8 %custom-call.31 = f32[1,128,128]{1,2,0:T(8,128)S(1)} custom-call(f32[1,128,128]{2,1,0:T(8,128)S(1)} %get-tuple-element.65), custom_call_target="InvertDiagBlocksLowerTriangular" | custom-call | tf_op jit(solution)/shard_map/jit(cholesky)/cholesky | solution.py:63
  766.0 11.7 %cholesky.377 = f32[128,128]{1,0:T(8,128)S(1)} custom-call(f32[128,128]{1,0:T(8,128)S(1)} %cholesky.443), custom_call_target="Cholesky" | custom-call | tf_op jit(solution)/shard_map/jit(cholesky)/cholesky | solution.py:63
  778.3 10.0 %custom-call.32 = f32[1,128,128]{1,2,0:T(8,128)S(1)} custom-call(f32[1,128,128]{2,1,0:T(8,128)S(1)} %get-tuple-element.62), custom_call_target="InvertDiagBlocksLowerTriangular" | custom-call | tf_op jit(solution)/shard_map/jit(cholesky)/cholesky | solution.py:63
  792.2 13.2 %cholesky.398 = f32[128,128]{1,0:T(8,128)} custom-call(f32[128,128]{1,0:T(8,128)} %cholesky.448), custom_call_target="Cholesky" | custom-call | tf_op jit(solution)/shard_map/jit(cholesky)/cholesky | solution.py:63
  806.9 11.3 %custom-call.33 = f32[1,128,128]{1,2,0:T(8,128)} custom-call(f32[1,128,128]{2,1,0:T(8,128)} %get-tuple-element.59), custom_call_target="InvertDiagBlocksLowerTriangular" | custom-call | tf_op jit(solution)/shard_map/jit(cholesky)/cholesky | solution.py:63
  821.3 11.7 %cholesky.415 = f32[128,128]{1,0:T(8,128)S(1)} custom-call(f32[128,128]{1,0:T(8,128)S(1)} %convolution_subtract_fusion.12), custom_call_target="Cholesky" | custom-call | tf_op jit(solution)/shard_map/jit(cholesky)/cholesky | solution.py:63
  839.2 2.3 select_select_fusion
  842.3 13.9 %while.5 = (s32[]{:T(128)}, f32[512,512]{1,0:T(8,128)}, s32[4,2]{0,1:T(2,128)S(1)}, f32[4,128,128]{2,1,0:T(8,128)}, s32[]{:T(128)}) while((s32[]{:T(128)}, f32[512,512]{1,0:T(8,128)}, s32[4,2]{0,1:T(2,128)S(1)}, f32[4,128,128]{2,1,0:T(8,128)}, s32[]{:T(128)}) %tuple.138), condition=%wide.while_cond.clone, body=%wide.while_body.clone.sunk | while | flops 2 | bytes 132705 | solution.py:65
  843.3 2.8 bitcast_dynamic-update-slice_fusion.5
  846.7 2.8 bitcast_dynamic-update-slice_fusion.5
  850.1 2.8 bitcast_dynamic-update-slice_fusion.5
  853.5 2.7 bitcast_dynamic-update-slice_fusion.5
  856.2 40.7 %custom-call.34 = f32[4,128,128]{1,2,0:T(8,128)} custom-call(f32[4,128,128]{2,1,0:T(8,128)} %get-tuple-element.31), custom_call_target="InvertDiagBlocksLowerTriangular" | custom-call | tf_op jit(solution)/shard_map/jit(_solve_triangular)/triangular_solve | solution.py:65
  908.7 2.8 convolution_negate_fusion
  911.6 8.0 fusion
  919.6 10.1 %all-reduce.11.cloned.1.call-done = f32[1024,1536]{1,0:T(8,128)} async-done(((f32[1024,1536]{1,0:T(8,128)}), f32[1024,1536]{1,0:T(8,128)}) %all-reduce.11.cloned.1.call-update) | async-done | bytes 6291472 | tf_op jit(solution)/shard_map/psum | solution.py:104
  929.7 15.2 %fusion.1 = f32[1024,1536]{1,0:T(8,128)S(1)} fusion(f32[1024,1536]{1,0:T(8,128)} %all-reduce.11.cloned.1.call-done, f32[512,512]{1,0:T(8,128)} %pad_maximum_fusion, f32[128,512]{1,0:T(8,128)} %copy-done.21, f32[128,512]{1,0:T(8,128)} %copy-done.19, f32[128,512]{1,0:T(8,128)} %copy-done.16, f32[128,512]{1,0:T(8,128)S(1)} %copy-done.10, ...), kind=kOutput, calls=%fused_computation.17 | convolution fusion | flops 9671016448 | bytes 15728640 | tf_op jit(solution)/shard_map/dot_general | solution.py:56
  944.9 7.2 convolution_subtract_fusion
  (176 shorter events, 90.1 us)
Async XLA Ops:
  12.6 94.0 %all-to-all-start = ((s32[16,1,152]{2,1,0:T(1,128)}), s32[16,1,152]{2,1,0:T(1,128)S(1)}, u32[]{:S(2)}, u32[]{:S(2)}) async-start(s32[16,1,152]{2,1,0:T(1,128)} %all_to_all.9), calls=%async_computation | async-start | bytes 32768 | tf_op jit(solution)/shard_map/all_to_all | solution.py:99
  70.7 14.2 %copy-start = (f32[512,1536]{1,0:T(8,128)}, f32[512,1536]{1,0:T(8,128)S(1)}, u32[]{:S(2)}) copy-start(f32[512,1536]{1,0:T(8,128)S(1)} %compare_select_fusion) | copy-start | bytes 9437188
  80.9 1.9 copy-start.8
  106.6 616.1 %all-to-all-start.1 = ((f32[16,152,1536]{2,1,0:T(8,128)}), f32[16,152,1536]{2,1,0:T(8,128)}, u32[]{:S(2)}, u32[]{:S(2)}) async-start(f32[16,152,1536]{2,1,0:T(8,128)} %broadcast_select_fusion), calls=%async_computation.1 | async-start | bytes 29884416 | tf_op jit(solution)/shard_map/all_to_all | solution.py:98
  113.3 387.5 %all-reduce.7.cloned.1.call-start = ((), (), s32[]{:S(2)}) async-start(), calls=%async_computation.2 | async-start | bytes 6291456 | tf_op jit(solution)/shard_map/psum | solution.py:94
  114.0 599.5 %all-reduce.9.cloned.1.call-start = ((), (), s32[]{:S(2)}) async-start(), calls=%async_computation.3 | async-start | bytes 4194304 | tf_op jit(solution)/shard_map/psum | solution.py:13
  114.2 541.7 %copy-start.4 = (f32[512,512]{1,0:T(8,128)}, f32[512,512]{1,0:T(8,128)S(1)}, u32[]{:S(2)}) copy-start(f32[512,512]{1,0:T(8,128)S(1)} %fusion.17) | copy-start | bytes 3145732
  503.9 22.7 %copy-start.18 = (f32[512,512]{1,0:T(8,128)}, f32[512,512]{1,0:T(8,128)S(1)}, u32[]{:S(2)}) copy-start(f32[512,512]{1,0:T(8,128)S(1)} %fusion.14) | copy-start | bytes 3145732
  527.6 121.8 %slice-start = ((f32[512,1536]{1,0:T(8,128)}), f32[512,1024]{1,0:T(8,128)S(1)}, s32[]{:S(2)}) async-start(f32[512,1536]{1,0:T(8,128)} %copy-done), calls=%async_computation.6 | async-start | bytes 4194304 | tf_op jit(solution)/shard_map/slice | solution.py:87
  650.9 2.7 copy-start.23
  650.9 260.7 %all-reduce.13.cloned.1.call-start = ((), (), s32[]{:S(2)}) async-start(), calls=%async_computation.5 | async-start | bytes 4194304 | tf_op jit(solution)/shard_map/psum | solution.py:13
  650.9 7.1 copy-start.13
  654.0 7.6 copy-start.6
  655.9 5.8 copy-start.11
  658.0 3.7 copy-start.14
  661.7 1.0 copy-start.2
  662.7 50.9 %copy-start.1 = (f32[512,1536]{1,0:T(8,128)S(1)}, f32[512,1536]{1,0:T(8,128)}, u32[]{:S(2)}) copy-start(f32[512,1536]{1,0:T(8,128)} %copy-done) | copy-start | bytes 9437188
  736.4 193.3 %all-reduce.11.cloned.1.call-start = ((), (), s32[]{:S(2)}) async-start(), calls=%async_computation.4 | async-start | bytes 12582912 | tf_op jit(solution)/shard_map/psum | solution.py:104
  738.4 1.0 copy-start.17
  765.3 0.7 copy-start.22
  897.0 5.4 copy-start.24
  897.0 5.8 copy-start.5
  899.2 7.6 copy-start.3
  899.2 7.6 copy-start.7
  899.2 7.6 copy-start.12
  899.2 7.6 copy-start.15
  900.8 7.9 copy-start.9
  902.8 5.9 copy-start.16
  904.7 4.0 copy-start.19
  906.8 1.9 copy-start.21
  911.6 18.1 %copy-start.10 = (f32[128,512]{1,0:T(8,128)S(1)}, f32[128,512]{1,0:T(8,128)}, u32[]{:S(2)}) copy-start(f32[128,512]{1,0:T(8,128)} %copy-done.9) | copy-start | bytes 786436
  929.7 15.2 %copy-start.20 = (f32[512,1024]{1,0:T(8,128)S(1)}, f32[512,1024]{1,0:T(8,128)}, u32[]{:S(2)}) copy-start(f32[512,1024]{1,0:T(8,128)} %fusion) | copy-start | bytes 6291460
Sparse Core Ops, SparseCore 0:
  118.9 381.9 all-reduce.6
  651.0 62.4 all-reduce.8
  736.5 65.7 all-reduce.12
  806.0 123.6 all-reduce.10

commit v2 on v1

--- a/solution.py
+++ b/solution.py
@@ -59,20 +59,32 @@
     )
 
 
-def cholesky_inverse(gram):
-    lower = jnp.linalg.cholesky(gram)
-    eye = jnp.eye(gram.shape[0], dtype=gram.dtype)
-    return jax.scipy.linalg.solve_triangular(lower, eye, lower=True)
-
-
-def gram_inverse_factor(g00, g10, g11):
-    i00 = cholesky_inverse(g00)
-    l10 = matmul(g10, i00.T)
-    i11 = cholesky_inverse(g11 - matmul(l10, l10.T))
-    i10 = -matmul(i11, matmul(l10, i00))
-    return jnp.concatenate(
-        [jnp.concatenate([i00, jnp.zeros_like(i00)], 1), jnp.concatenate([i10, i11], 1)], 0
-    )
+def inverse_factor(upper, size):
+    count = upper.shape[0] // size
+    eye = jnp.eye(size, dtype=upper.dtype)
+    done = jnp.zeros((upper.shape[0], 0), upper.dtype)
+    rest = upper
+    rows = []
+    for k in range(count):
+        lower = lax.linalg.cholesky(rest[:size, :size], symmetrize_input=False)
+        small = lax.linalg.triangular_solve(lower, eye, left_side=True, lower=True)
+        scaled = matmul(small, jnp.concatenate([rest[:size, size:], done[:size]], axis=1))
+        right = rest.shape[1] - size
+        rows.append(
+            jnp.concatenate(
+                [scaled[:, right:], small, jnp.zeros((size, right), upper.dtype)], axis=1
+            )
+        )
+        if right > 0:
+            terms = jnp.concatenate([scaled, small], axis=1)
+            taken = lax.dot_general(
+                scaled[:, :right], terms, (((0,), (0,)), ((), ())),
+                precision=lax.Precision.HIGHEST, preferred_element_type=jnp.float32,
+            )
+            rest = rest[size:, size:] - taken[:, :right]
+            fresh = jnp.zeros((right, size), upper.dtype)
+            done = jnp.concatenate([done[size:], fresh], axis=1) - taken[:, right:]
+    return jnp.concatenate(rows, axis=0)
 
 
 def shards(child_rows, row_map, stair):
@@ -84,31 +96,29 @@
     limits = jnp.take(stair, row_map // STAIR_BLOCK)
     masked = jnp.where(columns[None, :] >= limits[:, None], child_rows, jnp.zeros_like(child_rows))
 
-    own = masked[:, :wide]
-    left = matmul(own.T, own[:, :PANEL])
-    low = matmul(own[:, PANEL:].T, own[:, PANEL:])
+    sent_rows, sent_slots = pack_rows(masked, row_map, groups)
+    recv_slots = lax.all_to_all(sent_slots, "gr", split_axis=0, concat_axis=0, tiled=True)
+
+    panel = spread(masked[:, :wide], "gc", 0)
+    first, second = panel[:, :PANEL], panel[:, PANEL:]
+    local = high(panel, masked, ((0,), (0,)))
+    top = matmul(first.T, panel)
+    low = matmul(second.T, second)
+    left = jnp.concatenate([top[:, :PANEL], top[:, PANEL:]], axis=0)
     low = jnp.concatenate([low[:, :half], low[:, half:]], axis=0)
-    gram = jnp.concatenate([left, low], axis=1)
-    gram = jnp.where(lax.axis_index("gc") == 0, gram, jnp.zeros_like(gram))
-    gram, masked, own = lax.optimization_barrier((gram, masked, own))
-    gram = lax.psum(gram, ("gr", "gc"))
+    sums = lax.psum(jnp.concatenate([local, left, low], axis=1), "gr")
 
-    sent_rows, sent_slots = pack_rows(masked, row_map, groups)
-    recv_rows, recv_slots = (
-        lax.all_to_all(sent_rows, "gr", split_axis=0, concat_axis=0, tiled=True),
-        lax.all_to_all(sent_slots, "gr", split_axis=0, concat_axis=0, tiled=True),
-    )
-    own, gram = lax.optimization_barrier((own, gram))
-    panel = spread(own, "gc", 0)
-    local = high(panel, masked, ((0,), (0,)))
-    products = lax.psum(local, "gr")
-
+    sums, sent_rows = lax.optimization_barrier((sums, sent_rows))
+    recv_rows = lax.all_to_all(sent_rows, "gr", split_axis=0, concat_axis=0, tiled=True)
+    products = sums[:, :cols_dev]
+    gram = sums[:, cols_dev:]
     low = jnp.concatenate([gram[:PANEL, PANEL:], gram[PANEL:, PANEL:]], axis=1)
-    inverse = gram_inverse_factor(gram[:PANEL, :PANEL], gram[PANEL:, :PANEL], low)
+    top = jnp.concatenate([gram[:PANEL, :PANEL], gram[PANEL:, :PANEL]], axis=1)
+    low = jnp.concatenate([jnp.zeros_like(low), low], axis=1)
+    inverse = inverse_factor(jnp.concatenate([top, low], axis=0), STAIR_BLOCK)
 
     front = place_rows(recv_rows, recv_slots, rows_dev)
-    front_own, _ = lax.optimization_barrier((front[:, :wide], local))
-    front_panel = spread(front_own, "gc", 0)
+    front_panel = spread(front[:, :wide], "gc", 0)
     basis = high(front_panel, inverse, ((1,), (1,)))
     stacked = high(inverse, products, ((1,), (0,)))
     projected = front - high(basis, stacked, ((1,), (0,)))

time: 972 us -> 685 us (0.70)
  waiting for transfers between devices: 430 us -> 255 us
  other arithmetic: 320 us -> 264 us
  matrix products: 89.4 us -> 62.4 us
  local copies, waits for them, and re-layouts: 85.2 us -> 64.7 us
    psum x2 -> x1, waiting for transfers between devices: 384 us -> 99.9 us  [shards(): sums = lax.psum(jnp.concatenate([local, left, low], axis=1), 'gr')]
    psum x2, waiting for transfers between devices: 45.4 us -> 124 us  [spread(): return lax.psum(kept, axis)]
    another operation x37 -> x42, other arithmetic: 255 us -> 185 us  [the longest x24 99.8 us: inverse_factor(): lower = lax.linalg.cholesky(rest[:size, :size], symmetrize_input=False)]
    all_to_all x1, waiting for transfers between devices: 0.01 us -> 30.8 us  [shards(): lax.all_to_all(sent_rows, 'gr', split_axis=0, concat_axis=0, tiled=True)]
    another operation x26 -> x8, matrix products: 30.9 us -> 2.14 us  [inverse_factor(): small = lax.linalg.triangular_solve(lower, eye, left_side=True, lower=True)]
    another operation x37 -> x10, local copies, waits for them, and re-layouts: 29.1 us -> 0.84 us  [the longest x7 0.62 us: inverse_factor(): small = lax.linalg.triangular_solve(lower, eye, left_side=True, lower=True)]
    dot_general x0 -> x7, matrix products: none -> 12.9 us  [inverse_factor(): lax.dot_general(scaled[:, :right], terms, (((0,), (0,)), ((), ())), preci...]
  transfers between devices with their start and end apart: 6 -> 5, of which waited for: 3 -> 4; matrix products, arithmetic and copies ran while one was open for 47% -> 42% of each run, Pallas kernels for 0% -> 0%
where the time goes in v2:
time: 685 us; the launch traced here: 673 us
  other arithmetic  264 us (39%)
  waiting for transfers between devices  255 us (37%)
  local copies, waits for them, and re-layouts  64.7 us (9%)
  matrix products  62.4 us (9%)
  between operations  15.4 us (2%)
  starting transfers between devices  12.2 us (2%)
    psum x2, waiting for transfers between devices, spread(): return lax.psum(kept, axis)  124 us
    psum x1, waiting for transfers between devices, shards(): sums = lax.psum(jnp.concatenate([local, left, low], axis=1), 'gr')  99.9 us
    another operation x24, other arithmetic, inverse_factor(): lower = lax.linalg.cholesky(rest[:size, :size], symmetrize_input=False)  99.8 us
    another operation x16, other arithmetic, inverse_factor(): small = lax.linalg.triangular_solve(lower, eye, left_side=True, lower=True)  83.9 us
    select_n x1, other arithmetic, shards(): limits = jnp.take(stair, row_map // STAIR_BLOCK)  40.6 us
    dot_general x4, matrix products, high(): lax.dot_general(left, right, (contract, ((), ())), precision=lax.Precisio...  33.4 us
    all_to_all x1, waiting for transfers between devices, shards(): lax.all_to_all(sent_rows, 'gr', split_axis=0, concat_axis=0, tiled=True)  30.8 us
    dot_general x10, matrix products, matmul(): jnp.dot(left, right, precision=lax.Precision.HIGHEST, preferred_element_t...  14 us
  transfers between devices with their start and end apart: 5, of which 4 were waited for; matrix products, arithmetic and copies ran while one was open for 42% of the time, Pallas kernels for 0%

profile of v2, /device:TPU:1, one launch (start us, length us, event | category | flops | bytes accessed | tf_op | source)
XLA Modules:
  0.0 673.4 jit_solution(3320407137401549536)
XLA Ops:
  8.8 2.1 fusion.135
  10.9 2.1 fusion.134
  13.0 2.1 fusion.136
  15.0 40.6 %select_select_fusion.8 = s32[512]{0:T(512)S(1)} fusion(s32[512]{0:T(512)} %param.7, s32[]{:T(128)} %bitcast, s32[]{:T(128)} %bitcast.1, s32[]{:T(128)} %bitcast.2, s32[]{:T(128)} %bitcast.3, s32[]{:T(128)} %bitcast.4, s32[]{:T(128)} %bitcast.5, s32[]{:T(128)} %bitcast.6, s32[]{:T(128)} %bitcast.7, s32[]{:T(128)} %bitcast.8, s32[]{:T(128)} %bitcast.9, ...), kind=kLoop, calls=%fused_computation.189 | loop fusion | flops 75776 | bytes 4352 | tf_op jit(solution)/shard_map/jit(_take)/select_n | solution.py:96
  55.7 2.2 compare_select_fusion
  59.5 67.3 %all-reduce.11.cloned.1.call-done = f32[512,1024]{1,0:T(8,128)} async-done(((f32[512,1024]{1,0:T(8,128)}), f32[512,1024]{1,0:T(8,128)}) %all-reduce.11.cloned.1.call-update) | async-done | bytes 2097168 | tf_op jit(solution)/shard_map/psum | solution.py:13
  126.8 3.5 fusion.3
  130.4 3.6 fusion.5
  134.2 5.7 fusion.138
  139.9 7.1 %maximum_maximum_fusion = f32[1024,2304]{1,0:T(8,128)} fusion(f32[512,256]{1,0:T(8,128)S(1)} %get-tuple-element.17, f32[512,256]{1,0:T(8,128)S(1)} %get-tuple-element.16, f32[512,512]{1,0:T(8,128)S(1)} %get-tuple-element.15, f32[512,512]{1,0:T(8,128)S(1)} %get-tuple-element.14, f32[1024,1536]{1,0:T(8,128)S(1)} %fusion.138), kind=kLoop, calls=%fused_computation.5 | loop fusion | flops 9437184 | bytes 18874368 | tf_op jit(solution)/shard_map/concatenate | solution.py:109
  149.3 2.5 scatter_custom_fusion.1
  152.5 6.5 all-to-all-start
  159.0 2.5 scatter_custom_fusion
  161.6 10.0 %gather_fusion = f32[2432,1536]{1,0:T(8,128)} fusion(f32[512,1536]{1,0:T(8,128)S(1)} %compare_select_fusion, s32[3072]{0:T(1024)S(1)} %pad_clamp_fusion), kind=kCustom, calls=%fused_computation | custom fusion | bytes 29894144 | tf_op jit(solution)/shard_map/jit(_take)/gather | solution.py:30
  171.6 12.5 %broadcast_select_fusion = f32[16,152,1536]{2,1,0:T(8,128)} fusion(f32[16,152,1536]{2,1,0:T(8,128)} %bitcast.146, pred[16,152]{1,0:T(8,128)(4,1)S(1)} %broadcast_in_dim.83), kind=kLoop, calls=%fused_computation.6 | loop fusion | flops 3735552 | bytes 29886848 | tf_op jit(solution)/shard_map/jit(_take)/select_n | solution.py:30
  185.0 12.3 %scatter_custom_fusion.2 = s32[512]{0:T(512)S(1)} fusion(s32[2432]{0:T(1024)S(1)} %fusion.105, s32[2432]{0:T(1024)S(1)} %iota.147, s32[]{:T(128)} %constant.119.clone.1), kind=kCustom, calls=%fused_computation.200 | custom fusion | bytes 2052 | tf_op jit(solution)/shard_map/scatter | solution.py:46
  198.4 99.9 %all-reduce.13.cloned.1.call-done = f32[1024,2304]{1,0:T(8,128)} async-done(((f32[1024,2304]{1,0:T(8,128)}), f32[1024,2304]{1,0:T(8,128)}) %all-reduce.13.cloned.1.call-update) | async-done | bytes 9437200 | tf_op jit(solution)/shard_map/psum | solution.py:109
  300.9 5.1 all-to-all-start.1
  306.5 11.7 %custom-call.20 = f32[128,128]{1,0:T(8,128)S(1)} custom-call(f32[128,128]{1,0:T(8,128)S(1)} %slice.241), custom_call_target="Cholesky" | custom-call | tf_op jit(solution)/shard_map/cholesky/custom-call.1 | solution.py:69
  319.6 9.8 %custom-call.21 = f32[1,128,128]{1,2,0:T(8,128)S(1)} custom-call(f32[1,128,128]{2,1,0:T(8,128)S(1)} %fusion.84), custom_call_target="InvertDiagBlocksLowerTriangular" | custom-call | tf_op jit(solution)/shard_map/triangular_solve/custom-call.0 | solution.py:70
  330.2 3.1 fusion.7
  336.8 11.9 %custom-call.22 = f32[128,128]{1,0:T(8,128)S(1)} custom-call(f32[128,128]{1,0:T(8,128)S(1)} %slice.384), custom_call_target="Cholesky" | custom-call | tf_op jit(solution)/shard_map/cholesky/custom-call.1 | solution.py:69
  350.0 9.8 %custom-call.23 = f32[1,128,128]{1,2,0:T(8,128)S(1)} custom-call(f32[1,128,128]{2,1,0:T(8,128)S(1)} %fusion.85), custom_call_target="InvertDiagBlocksLowerTriangular" | custom-call | tf_op jit(solution)/shard_map/triangular_solve/custom-call.0 | solution.py:70
  361.9 2.7 fusion.11
  367.4 11.9 %custom-call.24 = f32[128,128]{1,0:T(8,128)S(1)} custom-call(f32[128,128]{1,0:T(8,128)S(1)} %slice.392), custom_call_target="Cholesky" | custom-call | tf_op jit(solution)/shard_map/cholesky/custom-call.1 | solution.py:69
  380.6 9.8 %custom-call.25 = f32[1,128,128]{1,2,0:T(8,128)S(1)} custom-call(f32[1,128,128]{2,1,0:T(8,128)S(1)} %fusion.86), custom_call_target="InvertDiagBlocksLowerTriangular" | custom-call | tf_op jit(solution)/shard_map/triangular_solve/custom-call.0 | solution.py:70
  392.1 2.3 fusion.15
  395.5 11.7 %custom-call.26 = f32[128,128]{1,0:T(8,128)S(1)} custom-call(f32[128,128]{1,0:T(8,128)S(1)} %slice.401), custom_call_target="Cholesky" | custom-call | tf_op jit(solution)/shard_map/cholesky/custom-call.1 | solution.py:69
  408.6 9.8 %custom-call.27 = f32[1,128,128]{1,2,0:T(8,128)S(1)} custom-call(f32[1,128,128]{2,1,0:T(8,128)S(1)} %fusion.87), custom_call_target="InvertDiagBlocksLowerTriangular" | custom-call | tf_op jit(solution)/shard_map/triangular_solve/custom-call.0 | solution.py:70
  420.4 1.8 fusion.19
  422.8 11.7 %custom-call.28 = f32[128,128]{1,0:T(8,128)S(1)} custom-call(f32[128,128]{1,0:T(8,128)S(1)} %slice.410), custom_call_target="Cholesky" | custom-call | tf_op jit(solution)/shard_map/cholesky/custom-call.1 | solution.py:69
  435.8 9.8 %custom-call.29 = f32[1,128,128]{1,2,0:T(8,128)S(1)} custom-call(f32[1,128,128]{2,1,0:T(8,128)S(1)} %fusion.88), custom_call_target="InvertDiagBlocksLowerTriangular" | custom-call | tf_op jit(solution)/shard_map/triangular_solve/custom-call.0 | solution.py:70
  448.4 11.9 %custom-call.30 = f32[128,128]{1,0:T(8,128)S(1)} custom-call(f32[128,128]{1,0:T(8,128)S(1)} %slice.419), custom_call_target="Cholesky" | custom-call | tf_op jit(solution)/shard_map/cholesky/custom-call.1 | solution.py:69
  461.7 9.8 %custom-call.31 = f32[1,128,128]{1,2,0:T(8,128)S(1)} custom-call(f32[1,128,128]{2,1,0:T(8,128)S(1)} %fusion.89), custom_call_target="InvertDiagBlocksLowerTriangular" | custom-call | tf_op jit(solution)/shard_map/triangular_solve/custom-call.0 | solution.py:70
  474.2 11.7 %custom-call.32 = f32[128,128]{1,0:T(8,128)S(1)} custom-call(f32[128,128]{1,0:T(8,128)S(1)} %get-tuple-element.21), custom_call_target="Cholesky" | custom-call | tf_op jit(solution)/shard_map/cholesky/custom-call.1 | solution.py:69
  487.2 10.0 %custom-call.33 = f32[1,128,128]{1,2,0:T(8,128)S(1)} custom-call(f32[1,128,128]{2,1,0:T(8,128)S(1)} %fusion.90), custom_call_target="InvertDiagBlocksLowerTriangular" | custom-call | tf_op jit(solution)/shard_map/triangular_solve/custom-call.0 | solution.py:70
  501.1 11.7 %custom-call.34 = f32[128,128]{1,0:T(8,128)S(1)} custom-call(f32[128,128]{1,0:T(8,128)S(1)} %slice_subtract_fusion.14), custom_call_target="Cholesky" | custom-call | tf_op jit(solution)/shard_map/cholesky/custom-call.1 | solution.py:69
  514.2 9.8 %custom-call.35 = f32[1,128,128]{1,2,0:T(8,128)S(1)} custom-call(f32[1,128,128]{2,1,0:T(8,128)S(1)} %fusion.91), custom_call_target="InvertDiagBlocksLowerTriangular" | custom-call | tf_op jit(solution)/shard_map/triangular_solve/custom-call.0 | solution.py:70
  526.1 1.8 maximum_dynamic-update-slice_fusion.5
  527.9 1.8 maximum_dynamic-update-slice_fusion.4
  533.7 30.8 %all-to-all-done.1 = f32[16,152,1536]{2,1,0:T(8,128)} async-done(((f32[16,152,1536]{2,1,0:T(8,128)}), f32[16,152,1536]{2,1,0:T(8,128)}, u32[]{:S(2)}, u32[]{:S(2)}) %all-to-all-start.1) | async-done | bytes 14942240 | tf_op jit(solution)/shard_map/all_to_all | solution.py:112
  564.5 10.0 %gather_fusion.1 = f32[512,1536]{1,0:T(8,128)} fusion(f32[2432,1536]{1,0:T(8,128)} %bitcast.83, s32[1024]{0:T(1024)S(1)} %copy-done.27), kind=kCustom, calls=%fused_computation.1 | custom fusion | bytes 6293504 | tf_op jit(solution)/shard_map/jit(_take)/gather | solution.py:48
  574.5 2.2 broadcast_select_fusion.1
  578.3 13.7 %fusion = f32[1024,1536]{1,0:T(8,128)S(1)} fusion(f32[1024,1024]{1,0:T(8,128)} %maximum_dynamic-update-slice_fusion, f32[1024,2304]{1,0:T(8,128)} %all-reduce.13.cloned.1.call-done), kind=kOutput, calls=%fused_computation.7 | convolution fusion | flops 9663676416 | bytes 16777216 | tf_op jit(solution)/shard_map/dot_general | solution.py:56
  592.0 2.7 copy-done.7
  595.4 57.0 %all-reduce.15.cloned.1.call-done = f32[512,1024]{1,0:T(8,128)} async-done(((f32[512,1024]{1,0:T(8,128)}), f32[512,1024]{1,0:T(8,128)}) %all-reduce.15.cloned.1.call-update) | async-done | bytes 2097168 | tf_op jit(solution)/shard_map/psum | solution.py:13
  652.4 6.8 %fusion.139 = f32[512,1024]{1,0:T(8,128)S(1)} fusion(f32[512,1024]{1,0:T(8,128)} %all-reduce.15.cloned.1.call-done, f32[1024,1024]{1,0:T(8,128)} %maximum_dynamic-update-slice_fusion), kind=kOutput, calls=%fused_computation.230 | convolution fusion | flops 3221225472 | bytes 8388608 | tf_op jit(solution)/shard_map/dot_general | solution.py:56
  659.1 7.2 %convolution_subtract_fusion = f32[512,1536]{1,0:T(8,128)} fusion(f32[512,1536]{1,0:T(8,128)S(1)} %broadcast_select_fusion.1, f32[512,1024]{1,0:T(8,128)S(1)} %fusion.139, f32[1024,1536]{1,0:T(8,128)S(1)} %copy-done.8), kind=kOutput, calls=%fused_computation.14 | convolution fusion | flops 4832624640 | bytes 14680064 | tf_op jit(solution)/shard_map/dot_general | solution.py:56
  (209 shorter events, 53.9 us)
Async XLA Ops:
  7.2 119.6 %all-reduce.11.cloned.1.call-start = ((), (), s32[]{:S(2)}) async-start(), calls=%async_computation.2 | async-start | bytes 4194304 | tf_op jit(solution)/shard_map/psum | solution.py:13
  59.4 238.9 %all-reduce.13.cloned.1.call-start = ((), (), s32[]{:S(2)}) async-start(), calls=%async_computation.3 | async-start | bytes 18874368 | tf_op jit(solution)/shard_map/psum | solution.py:109
  126.8 3.6 copy-start
  147.0 0.7 copy-start.28
  152.5 32.3 %all-to-all-start = ((s32[16,1,152]{2,1,0:T(1,128)}), s32[16,1,152]{2,1,0:T(1,128)S(1)}, u32[]{:S(2)}, u32[]{:S(2)}) async-start(s32[16,1,152]{2,1,0:T(1,128)} %all_to_all.9), calls=%async_computation | async-start | bytes 32768 | tf_op jit(solution)/shard_map/all_to_all | solution.py:100
  300.9 28.8 %copy-start.1 = (f32[512,512]{1,0:T(8,128)}, f32[512,512]{1,0:T(8,128)S(1)}, u32[]{:S(2)}) copy-start(f32[512,512]{1,0:T(8,128)S(1)} %get-tuple-element.10) | copy-start | bytes 3145732
  300.9 28.8 %copy-start.3 = (f32[512,512]{1,0:T(8,128)}, f32[512,512]{1,0:T(8,128)S(1)}, u32[]{:S(2)}) copy-start(f32[512,512]{1,0:T(8,128)S(1)} %get-tuple-element.11) | copy-start | bytes 3145732
  300.9 263.6 %all-to-all-start.1 = ((f32[16,152,1536]{2,1,0:T(8,128)}), f32[16,152,1536]{2,1,0:T(8,128)}, u32[]{:S(2)}, u32[]{:S(2)}) async-start(f32[16,152,1536]{2,1,0:T(8,128)} %broadcast_select_fusion), calls=%async_computation.1 | async-start | bytes 29884416 | tf_op jit(solution)/shard_map/all_to_all | solution.py:112
  306.1 346.3 %all-reduce.15.cloned.1.call-start = ((), (), s32[]{:S(2)}) async-start(), calls=%async_computation.4 | async-start | bytes 4194304 | tf_op jit(solution)/shard_map/psum | solution.py:13
  333.3 2.3 copy-start.2
  333.3 2.3 copy-start.4
  360.2 4.5 copy-start.15
  360.2 4.3 copy-start.14
  361.8 2.9 copy-start.11
  366.0 1.4 copy-start.5
  366.0 28.4 %copy-start.10 = (f32[640,256]{1,0:T(8,128)S(1)}, f32[640,256]{1,0:T(8,128)}, u32[]{:S(2)}) copy-start(f32[640,256]{1,0:T(8,128)} %slice.403) | copy-start | bytes 1966084
  390.8 3.7 copy-start.21
  392.1 2.5 copy-start.6
  394.5 1.0 copy-start.9
  395.5 26.8 %slice-start = ((f32[640,384]{1,0:T(8,128)}), f32[512,384]{1,0:T(8,128)S(1)}, s32[]{:S(2)}) async-start(f32[640,384]{1,0:T(8,128)} %copy-done.9), calls=%async_computation.5 | async-start | bytes 1572864 | tf_op jit(solution)/shard_map/slice | solution.py:86
  418.7 1.7 copy-start.19
  446.0 0.6 copy-start.23
  446.6 1.7 copy-start.12
  471.9 25.6 %copy-start.17 = (f32[128,128]{1,0:T(8,128)}, f32[128,128]{1,0:T(8,128)S(1)}, u32[]{:S(2)}) copy-start(f32[128,128]{1,0:T(8,128)S(1)} %copy.27) | copy-start | bytes 196612
  472.5 25.8 %copy-start.13 = (f32[128,896]{1,0:T(8,128)}, f32[128,896]{1,0:T(8,128)S(1)}, u32[]{:S(2)}) copy-start(f32[128,896]{1,0:T(8,128)S(1)} %fusion.54) | copy-start | bytes 1376260
  497.4 0.6 copy-start.25
  498.1 0.8 copy-start.26
  498.1 27.1 %slice-start.1 = ((f32[128,896]{1,0:T(8,128)}), f32[128,128]{1,0:T(8,128)S(1)}, s32[]{:S(2)}) async-start(f32[128,896]{1,0:T(8,128)} %copy-done.11), calls=%async_computation.6 | async-start | bytes 131072 | tf_op jit(solution)/shard_map/slice | solution.py:75
  498.1 27.1 %copy-start.16 = (f32[128,128]{1,0:T(8,128)S(1)}, f32[128,128]{1,0:T(8,128)}, u32[]{:S(2)}) copy-start(f32[128,128]{1,0:T(8,128)} %copy-done.15) | copy-start | bytes 196612
  498.2 27.9 %copy-start.22 = (f32[128,128]{1,0:T(8,128)S(1)}, f32[128,128]{1,0:T(8,128)}, u32[]{:S(2)}) copy-start(f32[128,128]{1,0:T(8,128)} %copy-done.21) | copy-start | bytes 196612
  498.2 29.7 %copy-start.20 = (f32[128,128]{1,0:T(8,128)S(1)}, f32[128,128]{1,0:T(8,128)}, u32[]{:S(2)}) copy-start(f32[128,128]{1,0:T(8,128)} %copy-done.19) | copy-start | bytes 196612
  498.3 31.4 %slice-start.2 = ((f32[128,896]{1,0:T(8,128)}), f32[128,512]{1,0:T(8,128)S(1)}, s32[]{:S(2)}) async-start(f32[128,896]{1,0:T(8,128)} %copy-done.12), calls=%async_computation.7 | async-start | bytes 524288 | tf_op jit(solution)/shard_map/slice | solution.py:75
  498.3 31.4 %copy-start.24 = (f32[128,128]{1,0:T(8,128)S(1)}, f32[128,128]{1,0:T(8,128)}, u32[]{:S(2)}) copy-start(f32[128,128]{1,0:T(8,128)} %copy-done.23) | copy-start | bytes 196612
  498.9 31.6 %slice-start.3 = ((f32[128,896]{1,0:T(8,128)}), f32[128,640]{1,0:T(8,128)S(1)}, s32[]{:S(2)}) async-start(f32[128,896]{1,0:T(8,128)} %copy-done.13), calls=%async_computation.8 | async-start | bytes 655360 | tf_op jit(solution)/shard_map/slice | solution.py:75
  498.9 31.6 %copy-start.18 = (f32[128,128]{1,0:T(8,128)S(1)}, f32[128,128]{1,0:T(8,128)}, u32[]{:S(2)}) copy-start(f32[128,128]{1,0:T(8,128)} %copy-done.17) | copy-start | bytes 196612
  527.9 36.6 %copy-start.27 = (s32[1024]{0:T(1024)S(1)}, s32[1024]{0:T(1024)}, u32[]{:S(2)}) copy-start(s32[1024]{0:T(1024)} %pad_clamp_fusion.1) | copy-start | bytes 12292
  564.5 10.0 %copy-start.29 = (pred[512]{0:T(512)(128)(4,1)S(1)}, pred[512]{0:T(512)(128)(4,1)}, u32[]{:S(2)}) copy-start(pred[512]{0:T(512)(128)(4,1)} %compare_and_fusion.1) | copy-start | bytes 1540
  592.0 2.7 copy-start.7
  652.4 6.8 %copy-start.8 = (f32[1024,1536]{1,0:T(8,128)S(1)}, f32[1024,1536]{1,0:T(8,128)}, u32[]{:S(2)}) copy-start(f32[1024,1536]{1,0:T(8,128)} %copy-done.7) | copy-start | bytes 18874372
Sparse Core Ops, SparseCore 0:
  59.5 67.2 all-reduce.10
  147.2 151.1 all-reduce.12
  578.4 73.9 all-reduce.14
